TPU v7x, 32 devices: a whole 2x2x4 slice. The times are simulated.
32 devices in a mesh: dp: 16 (over z, y, x), space: 2 (over core).
Axes of the slice: x: 2, y: 2, z: 4, core: 2. Of those that a mesh axis runs over, the one named last changes fastest.
Arguments:
- images: bfloat16 [16, 16, 288, 256], P('dp', 'space'), may hold values from -12 to 12
- w_reduce: bfloat16 [256, 64], replicated, may hold values from -0.375 to 0.375
- w_dilated: bfloat16 [3, 3, 64, 64], replicated, may hold values from -0.25 to 0.25
- w_expand: bfloat16 [64, 256], replicated, may hold values from -0.75 to 0.75
- gain_one: float32 [64], replicated, may hold values from 0.25 to 1.75
- shift_one: float32 [64], replicated, may hold values from -3 to 3
- gain_two: float32 [64], replicated, may hold values from 0.25 to 1.75
- shift_two: float32 [64], replicated, may hold values from -3 to 3
- gain_three: float32 [256], replicated, may hold values from 0.25 to 1.75
- shift_three: float32 [256], replicated, may hold values from -3 to 3
- cotangent: bfloat16 [16, 16, 288, 256], P('dp', 'space'), may hold values from -6 to 6
Outputs:
- result: bfloat16 [16, 16, 288, 256], P('dp', 'space')
- grad_images: bfloat16 [16, 16, 288, 256], P('dp', 'space')
- grad_reduce: float32 [256, 64], replicated
- grad_dilated: float32 [3, 3, 64, 64], replicated
- grad_expand: float32 [64, 256], replicated
- grad_gain_one: float32 [64], replicated
- grad_shift_one: float32 [64], replicated
- grad_gain_two: float32 [64], replicated
- grad_shift_two: float32 [64], replicated
- grad_gain_three: float32 [256], replicated
- grad_shift_three: float32 [256], replicated
All inputs are finite; a program needn't handle non-finite values.
Results may differ from a plain program's by a relative error of at most 0.012.
Values may be sent and summed in bfloat16 or wider, within the bound.
No kernel may reach another device: no remote copies, remote signals or barrier semaphores. Data moves between devices by JAX's collectives and lax.ppermute only.
A program may use at most 64 MiB of HBM per device.

v0:
```python
import jax
import jax.numpy as jnp
from jax import lax
from jax.sharding import PartitionSpec as P

epsilon = 1e-05


def extended(block, sides, width):
    for axis, dim in sides:
        count = lax.axis_size(axis)
        forward = [(i, i + 1) for i in range(count - 1)]
        backward = [(target, source) for source, target in forward]
        low = lax.ppermute(
            lax.slice_in_dim(block, block.shape[dim] - width, None, axis=dim), axis, forward
        )
        high = lax.ppermute(lax.slice_in_dim(block, 0, width, axis=dim), axis, backward)
        block = jnp.concatenate([low, block, high], axis=dim)
    return block


def smooth_act(value):
    return value * jax.nn.sigmoid(value)


def smooth_slope(value):
    sig = jax.nn.sigmoid(value)
    return sig * (1.0 + value * (1.0 - sig))


def normalize(pre, gain, shift, count):
    average = lax.psum(jnp.sum(pre, 0), "space") / count
    centred = pre - average
    variance = lax.psum(jnp.sum(centred * centred, 0), "space") / count
    inv_std = lax.rsqrt(variance + epsilon)
    normed = centred * inv_std
    return (normed, inv_std, gain * normed + shift)


def backnorm(grad, normed, inv_std, gain, count):
    local_sum = jnp.sum(grad, 0)
    local_cross = jnp.sum(grad * normed, 0)
    grad_sum, grad_cross = lax.psum((local_sum, local_cross), "space")
    back = (gain * inv_std * (grad - grad_sum / count - normed * grad_cross / count)).astype(
        jnp.bfloat16
    )
    return (back, local_cross, local_sum)


def dilated(padded, kernel, rows, cols):
    output = jnp.zeros((rows * cols, kernel.shape[3]), jnp.float32)
    for tap_row in range(3):
        for tap_col in range(3):
            window = padded[
                2 * tap_row : 2 * tap_row + rows, 2 * tap_col : 2 * tap_col + cols
            ].reshape(rows * cols, -1)
            output = output + jnp.dot(
                window, kernel[tap_row, tap_col], preferred_element_type=jnp.float32
            )
    return output


def contract(left, right):
    return lax.dot_general(
        left, right, (((0,), (0,)), ((), ())), preferred_element_type=jnp.float32
    )


def shards(
    images,
    w_reduce,
    w_dilated,
    w_expand,
    gain_one,
    shift_one,
    gain_two,
    shift_two,
    gain_three,
    shift_three,
    cotangent,
):
    rows, cols, chans = (images.shape[1], images.shape[2], images.shape[3])
    mids = w_reduce.shape[1]
    pixels = rows * cols
    count = float(pixels * lax.axis_size("space"))
    flat_in = images.reshape(pixels, chans)
    pre_one = jnp.dot(flat_in, w_reduce, preferred_element_type=jnp.float32)
    normed_one, istd_one, out_one = normalize(pre_one, gain_one, shift_one, count)
    act_one = smooth_act(out_one).astype(jnp.bfloat16)
    edged_one = extended(act_one.reshape(rows, cols, mids), (("space", 0),), 2)
    padded_one = jnp.pad(edged_one, ((0, 0), (2, 2), (0, 0)))
    pre_two = dilated(padded_one, w_dilated, rows, cols)
    normed_two, istd_two, out_two = normalize(pre_two, gain_two, shift_two, count)
    act_two = smooth_act(out_two).astype(jnp.bfloat16)
    pre_three = jnp.dot(act_two, w_expand, preferred_element_type=jnp.float32)
    normed_three, istd_three, out_three = normalize(pre_three, gain_three, shift_three, count)
    summed = out_three + flat_in.astype(jnp.float32)
    result = smooth_act(summed).astype(jnp.bfloat16)
    grad_three = cotangent.reshape(pixels, chans).astype(jnp.float32) * smooth_slope(summed)
    dh_three, gg_three, gs_three = backnorm(grad_three, normed_three, istd_three, gain_three, count)
    gw_expand = contract(act_two, dh_three)
    back_two = lax.dot_general(
        dh_three, w_expand, (((1,), (1,)), ((), ())), preferred_element_type=jnp.float32
    )
    grad_two = back_two * smooth_slope(out_two)
    dh_two, gg_two, gs_two = backnorm(grad_two, normed_two, istd_two, gain_two, count)
    taps = []
    for tap_row in range(3):
        for tap_col in range(3):
            window = padded_one[
                2 * tap_row : 2 * tap_row + rows, 2 * tap_col : 2 * tap_col + cols
            ].reshape(pixels, mids)
            taps.append(contract(window, dh_two))
    gw_dilated = jnp.stack(taps).reshape(3, 3, mids, mids)
    edged_back = extended(dh_two.reshape(rows, cols, mids), (("space", 0),), 2)
    padded_back = jnp.pad(edged_back, ((0, 0), (2, 2), (0, 0)))
    flipped = jnp.transpose(w_dilated[::-1, ::-1], (0, 1, 3, 2))
    grad_one = dilated(padded_back, flipped, rows, cols) * smooth_slope(out_one)
    dh_one, gg_one, gs_one = backnorm(grad_one, normed_one, istd_one, gain_one, count)
    gw_reduce = contract(flat_in, dh_one)
    back_in = lax.dot_general(
        dh_one, w_reduce, (((1,), (1,)), ((), ())), preferred_element_type=jnp.float32
    )
    grad_images = (back_in + grad_three).astype(jnp.bfloat16).reshape(1, rows, cols, chans)
    batch = float(lax.axis_size("dp"))
    parts_list = (
        gw_reduce,
        gw_dilated,
        gw_expand,
        gg_one,
        gs_one,
        gg_two,
        gs_two,
        gg_three,
        gs_three,
    )
    flat_grads = jnp.concatenate([item.reshape(-1) for item in parts_list])
    length = flat_grads.shape[0]
    groups = lax.axis_size("space")
    padded_len = (length + groups - 1) // groups * groups
    flat_grads = jnp.pad(flat_grads, (0, padded_len - length))
    share = lax.psum_scatter(
        flat_grads.astype(jnp.bfloat16), "space", scatter_dimension=0, tiled=True
    ).astype(jnp.float32)
    share = lax.psum(share, "dp")
    whole = lax.all_gather(share.astype(jnp.bfloat16), "space", axis=0, tiled=True).astype(
        share.dtype
    )
    summed_parts = []
    offset = 0
    for item in parts_list:
        summed_parts.append(whole[offset : offset + item.size].reshape(item.shape))
        offset = offset + item.size
    grads = [item / batch for item in summed_parts]
    return (
        result.reshape(1, rows, cols, chans),
        grad_images,
        grads[0],
        grads[1],
        grads[2],
        grads[3],
        grads[4],
        grads[5],
        grads[6],
        grads[7],
        grads[8],
    )


def solution(mesh):
    placed = (
        P("dp", "space", None, None),
        P(),
        P(),
        P(),
        P(),
        P(),
        P(),
        P(),
        P(),
        P(),
        P("dp", "space", None, None),
    )
    return jax.shard_map(
        shards,
        mesh=mesh,
        in_specs=placed,
        out_specs=(
            P("dp", "space", None, None),
            P("dp", "space", None, None),
            P(),
            P(),
            P(),
            P(),
            P(),
            P(),
            P(),
            P(),
            P(),
        ),
        check_vma=False,
    )
```

profile of v0, /device:TPU:0, one launch (start us, length us, event | category | flops | bytes accessed | tf_op | source)
XLA Modules:
  0.0 222.0 jit_solution(6507126635642277111)
XLA Ops:
  7.3 1.9 fusion.59
  9.2 2.6 %psum.91 = f32[64]{0:T(128)S(1)} all-reduce(f32[64]{0:T(128)S(1)} %get-tuple-element.81), channel_id=1, replica_groups=mesh['dp'=16,'space'=2] {'space'}, use_global_device_ids=true, to_apply=%region_1.0 | all-reduce | flops 64 | bytes 512 | tf_op jit(solution)/shard_map/psum | solution.py:32
  12.1 2.5 %psum.92 = f32[64]{0:T(128)S(1)} all-reduce(f32[64]{0:T(128)S(1)} %multiply_reduce_fusion.5), channel_id=1, replica_groups=mesh['dp'=16,'space'=2] {'space'}, use_global_device_ids=true, to_apply=%region_3.0 | all-reduce | flops 64 | bytes 512 | tf_op jit(solution)/shard_map/psum | solution.py:34
  16.3 2.3 %collective-permute-start = (bf16[2,288,64]{1,0,2:T(2,128)(2,1)S(1)}, bf16[2,288,64]{1,0,2:T(2,128)(2,1)S(1)}, u32[]{:S(2)}, u32[]{:S(2)}) collective-permute-start(bf16[2,288,64]{1,0,2:T(2,128)(2,1)S(1)} %slice.191), channel_id=1, source_target_pairs={{0,1},{2,3},{4,5},{6,7},{8,9},{10,11},{12,13},{14,15},{16,17},{18,... | collective-permute-start | bytes 221192 | tf_op jit(solution)/shard_map/ppermute | solution.py:14
  18.7 1.3 collective-permute-start.1
  22.6 1.0 select_maximum_fusion.2
  23.6 1.8 fusion.56
  26.0 1.1 pad_maximum_fusion.2
  27.5 1.4 reshape.163
  28.9 1.4 reshape.164
  30.4 1.0 convolution_add_fusion.14
  32.4 1.1 convolution_add_fusion.12
  34.6 1.3 reshape.165
  36.6 1.0 fusion.28
  37.6 1.3 reshape.167
  38.9 1.0 convolution_add_fusion.10
  40.0 1.0 convolution_add_fusion.9
  41.1 1.1 fusion.60
  42.2 3.3 %psum.93 = f32[64]{0:T(128)S(1)} all-reduce(f32[64]{0:T(128)S(1)} %get-tuple-element.83), channel_id=1, replica_groups=mesh['dp'=16,'space'=2] {'space'}, use_global_device_ids=true, to_apply=%region_5.6 | all-reduce | flops 64 | bytes 512 | tf_op jit(solution)/shard_map/psum | solution.py:32
  45.7 2.5 %psum.94 = f32[64]{0:T(128)S(1)} all-reduce(f32[64]{0:T(128)S(1)} %multiply_reduce_fusion.4), channel_id=1, replica_groups=mesh['dp'=16,'space'=2] {'space'}, use_global_device_ids=true, to_apply=%region_7.8 | all-reduce | flops 64 | bytes 512 | tf_op jit(solution)/shard_map/psum | solution.py:34
  48.2 1.9 fusion.61
  50.1 2.5 %psum.95 = f32[256]{0:T(256)S(1)} all-reduce(f32[256]{0:T(256)S(1)} %get-tuple-element.85), channel_id=1, replica_groups=mesh['dp'=16,'space'=2] {'space'}, use_global_device_ids=true, to_apply=%region_9.10 | all-reduce | flops 256 | bytes 2048 | tf_op jit(solution)/shard_map/psum | solution.py:32
  52.9 2.6 %psum.96 = f32[256]{0:T(256)S(1)} all-reduce(f32[256]{0:T(256)S(1)} %multiply_reduce_fusion.1), channel_id=1, replica_groups=mesh['dp'=16,'space'=2] {'space'}, use_global_device_ids=true, to_apply=%region_11.12 | all-reduce | flops 256 | bytes 2048 | tf_op jit(solution)/shard_map/psum | solution.py:34
  55.6 5.1 %fusion.52 = (f32[256]{0:T(256)S(1)}, f32[256]{0:T(256)S(1)}, f32[2304,256]{1,0:T(8,128)}, bf16[2304,256]{1,0:T(8,128)(2,1)}) fusion(f32[256]{0:T(256)S(1)} %get-tuple-element.76, f32[2304,256]{1,0:T(8,128)S(1)} %get-tuple-element.86, f32[256]{0:T(256)S(1)} %broadcast_multiply_fusion.1, bf16[1,8,288,256]{3,2,1,0:T(8,128)(2,1)} %param.11, ...), kind=kLoop, calls=%fused_computation.141 | loop fusion | flops 11795968 | bytes 8263680 | tf_op jit(solution)/shard_map/reduce_sum | solution.py:41
  60.6 2.5 %all-reduce.5 = (f32[256]{0:T(256)S(1)}, f32[256]{0:T(256)S(1)}) all-reduce(f32[256]{0:T(256)S(1)} %get-tuple-element.34, f32[256]{0:T(256)S(1)} %get-tuple-element.33), channel_id=1, replica_groups=mesh['dp'=16,'space'=2] {'space'}, use_global_device_ids=true, to_apply=%region_15.16 | all-reduce | flops 512 | bytes 4096 | tf_op jit(solution)/shard_map/psum | solution.py:43
  63.1 2.3 %multiply_convert_fusion = bf16[2304,256]{1,0:T(8,128)(2,1)S(1)} fusion(f32[2304,256]{1,0:T(8,128)} %get-tuple-element.45, f32[2304,256]{1,0:T(8,128)S(1)} %get-tuple-element.86, f32[256]{0:T(256)S(1)} %get-tuple-element.43, f32[256]{0:T(256)S(1)} %broadcast_multiply_fusion, f32[256]{0:T(256)S(1)} %get-tuple-element.75, f32[256]{0:T(256)S(1)} %get-tuple-element.76, ...), kind=kLoop, calls=%fused_computation.23 | loop fusion | flops 4718592 | bytes 5903360 | tf_op jit(solution)/shard_map/convert_element_type | solution.py:44
  65.8 1.4 fusion.54
  67.3 2.6 %all-reduce.4 = (f32[64]{0:T(128)S(1)}, f32[64]{0:T(128)S(1)}) all-reduce(f32[64]{0:T(128)S(1)} %get-tuple-element.38, f32[64]{0:T(128)S(1)} %get-tuple-element.37), channel_id=1, replica_groups=mesh['dp'=16,'space'=2] {'space'}, use_global_device_ids=true, to_apply=%region_19.20 | all-reduce | flops 128 | bytes 1024 | tf_op jit(solution)/shard_map/psum | solution.py:43
  69.9 1.5 multiply_convert_fusion.3
  73.6 2.3 %collective-permute-start.2 = (bf16[2,288,64]{1,0,2:T(2,128)(2,1)S(1)}, bf16[2,288,64]{1,0,2:T(2,128)(2,1)S(1)}, u32[]{:S(2)}, u32[]{:S(2)}) collective-permute-start(bf16[2,288,64]{1,0,2:T(2,128)(2,1)S(1)} %slice.212), channel_id=1, source_target_pairs={{0,1},{2,3},{4,5},{6,7},{8,9},{10,11},{12,13},{14,15},{16,17},{18,... | collective-permute-start | bytes 221192 | tf_op jit(solution)/shard_map/ppermute | solution.py:14
  76.0 1.3 collective-permute-start.3
  81.0 1.1 pad_maximum_fusion
  82.2 1.0 reshape.172
  83.2 1.0 select_maximum_fusion
  84.3 1.5 fusion.55
  85.8 1.3 reshape.171
  87.1 1.0 reshape.173
  88.1 1.0 reshape.174
  89.4 1.2 convolution_add_fusion.7
  93.3 1.4 fusion.53
  94.8 3.6 %all-reduce.3 = (f32[64]{0:T(128)S(1)}, f32[64]{0:T(128)S(1)}) all-reduce(f32[64]{0:T(128)S(1)} %get-tuple-element.36, f32[64]{0:T(128)S(1)} %get-tuple-element.35), channel_id=1, replica_groups=mesh['dp'=16,'space'=2] {'space'}, use_global_device_ids=true, to_apply=%region_23.24 | all-reduce | flops 128 | bytes 1024 | tf_op jit(solution)/shard_map/psum | solution.py:43
  98.4 1.4 multiply_convert_fusion.2
  99.9 1.6 fusion.5
  101.7 6.3 %concatenate.28 = bf16[70400]{0:T(1024)(128)(2,1)} concatenate(bf16[16384]{0:T(1024)(128)(2,1)S(1)} %reshape.180, bf16[36864]{0:T(1024)(128)(2,1)S(1)} %copy-done.27, bf16[16384]{0:T(1024)(128)(2,1)S(1)} %bitcast.206, bf16[64]{0:T(256)(128)(2,1)S(1)} %convert.77, bf16[64]{0:T(256)(128)(2,1)S(1)} %convert.78, bf16[64]{0:T(256)(128)(2,1)S(1)} %copy-done.39, ...), dimensions={0} | concatenate | bytes 281600 | tf_op jit(solution)/shard_map/concatenate | solution.py:137
  108.1 1.5 fusion
  109.6 18.9 %all-reduce.9.cloned.1.call-done = bf16[70400]{0:T(1024)(128)(2,1)} async-done(((bf16[70400]{0:T(1024)(128)(2,1)}), bf16[70400]{0:T(1024)(128)(2,1)}) %all-reduce.9.cloned.1.call-update) | async-done | bytes 140816
  129.5 78.9 %all-reduce.10 = bf16[35200]{0:T(1024)(128)(2,1)S(1)} all-reduce(f32[35200]{0:T(1024)S(1)} %dynamic-slice_convert_fusion), channel_id=1, replica_groups=mesh['dp'=16,'space'=2] {'dp'}, use_global_device_ids=true, to_apply=%region_25.26 | all-reduce | flops 35200 | bytes 211200 | tf_op jit(solution)/shard_map/psum | solution.py:145
  208.5 2.0 all-gather
  (171 shorter events, 23.3 us)
Async XLA Ops:
  7.2 41.0 %copy-start = (bf16[64,256]{1,0:T(8,128)(2,1)S(1)}, bf16[64,256]{1,0:T(8,128)(2,1)}, u32[]{:S(2)}) copy-start(bf16[64,256]{1,0:T(8,128)(2,1)} %param.14) | copy-start | bytes 98308
  7.2 13.4 %copy-start.45 = (u32[32]{0:T(128)S(1)}, u32[32]{0:T(128)}, u32[]{:S(2)}) copy-start(u32[32]{0:T(128)} %constant.51) | copy-start | bytes 388
  7.2 7.3 %copy-start.34 = (f32[64]{0:T(128)S(1)}, f32[64]{0:T(128)}, u32[]{:S(2)}) copy-start(f32[64]{0:T(128)} %param.15) | copy-start | bytes 772
  7.2 8.4 %copy-start.37 = (f32[64]{0:T(128)S(1)}, f32[64]{0:T(128)}, u32[]{:S(2)}) copy-start(f32[64]{0:T(128)} %param.16) | copy-start | bytes 772
  7.2 14.6 %copy-start.25 = (bf16[3,3,64,64]{3,2,1,0:T(8,128)(2,1)S(1)}, bf16[3,3,64,64]{3,2,1,0:T(8,128)(2,1)}, u32[]{:S(2)}) copy-start(bf16[3,3,64,64]{3,2,1,0:T(8,128)(2,1)} %param.13) | copy-start | bytes 221188
  7.2 121.3 %all-reduce.9.cloned.1.call-start = ((), (), s32[]{:S(2)}) async-start(), calls=%async_computation | async-start | bytes 282624
  11.8 3.2 %copy-start.29 = (f32[64]{0:T(128)}, f32[64]{0:T(128)S(1)}, u32[]{:S(2)}) copy-start(f32[64]{0:T(128)S(1)} %broadcast_multiply_fusion.5) | copy-start | bytes 772
  16.3 6.3 %collective-permute-start = (bf16[2,288,64]{1,0,2:T(2,128)(2,1)S(1)}, bf16[2,288,64]{1,0,2:T(2,128)(2,1)S(1)}, u32[]{:S(2)}, u32[]{:S(2)}) collective-permute-start(bf16[2,288,64]{1,0,2:T(2,128)(2,1)S(1)} %slice.191), channel_id=1, source_target_pairs={{0,1},{2,3},{4,5},{6,7},{8,9},{10,11},{12,13},{14,15},{16,17},{18,... | collective-permute-start | bytes 221192 | tf_op jit(solution)/shard_map/ppermute | solution.py:14
  18.7 3.9 %collective-permute-start.1 = (bf16[2,288,64]{1,0,2:T(2,128)(2,1)S(1)}, bf16[2,288,64]{1,0,2:T(2,128)(2,1)S(1)}, u32[]{:S(2)}, u32[]{:S(2)}) collective-permute-start(bf16[2,288,64]{1,0,2:T(2,128)(2,1)S(1)} %slice.193), channel_id=1, source_target_pairs={{1,0},{3,2},{5,4},{7,6},{9,8},{11,10},{13,12},{15,14},{17,16},{19,... | collective-permute-start | bytes 221192 | tf_op jit(solution)/shard_map/ppermute | solution.py:17
  25.7 5.7 %copy-start.9 = (bf16[2304,64]{0,1:T(8,128)(2,1)}, bf16[2304,64]{0,1:T(8,128)(2,1)S(1)}, u32[]{:S(2)}) copy-start(bf16[2304,64]{0,1:T(8,128)(2,1)S(1)} %reshape.161) | copy-start | bytes 884740
  27.5 6.1 %copy-start.15 = (bf16[2304,64]{0,1:T(8,128)(2,1)}, bf16[2304,64]{0,1:T(8,128)(2,1)S(1)}, u32[]{:S(2)}) copy-start(bf16[2304,64]{0,1:T(8,128)(2,1)S(1)} %reshape.162) | copy-start | bytes 884740
  28.9 4.6 %copy-start.13 = (bf16[2304,64]{0,1:T(8,128)(2,1)}, bf16[2304,64]{0,1:T(8,128)(2,1)S(1)}, u32[]{:S(2)}) copy-start(bf16[2304,64]{0,1:T(8,128)(2,1)S(1)} %reshape.163) | copy-start | bytes 884740
  30.4 4.2 %copy-start.11 = (bf16[2304,64]{0,1:T(8,128)(2,1)}, bf16[2304,64]{0,1:T(8,128)(2,1)S(1)}, u32[]{:S(2)}) copy-start(bf16[2304,64]{0,1:T(8,128)(2,1)S(1)} %reshape.164) | copy-start | bytes 884740
  32.4 3.8 %copy-start.21 = (bf16[8,288,64]{1,0,2:T(8,128)(2,1)S(1)}, bf16[8,288,64]{1,0,2:T(8,128)(2,1)}, u32[]{:S(2)}) copy-start(bf16[8,288,64]{1,0,2:T(8,128)(2,1)} %get-tuple-element.58) | copy-start | bytes 884740
  35.9 5.2 %copy-start.19 = (bf16[2304,64]{0,1:T(8,128)(2,1)}, bf16[2304,64]{0,1:T(8,128)(2,1)S(1)}, u32[]{:S(2)}) copy-start(bf16[2304,64]{0,1:T(8,128)(2,1)S(1)} %reshape.165) | copy-start | bytes 884740
  36.2 3.8 %copy-start.17 = (bf16[2304,64]{0,1:T(8,128)(2,1)}, bf16[2304,64]{0,1:T(8,128)(2,1)S(1)}, u32[]{:S(2)}) copy-start(bf16[2304,64]{0,1:T(8,128)(2,1)S(1)} %reshape.166) | copy-start | bytes 884740
  36.5 3.4 %copy-start.7 = (bf16[2304,64]{0,1:T(8,128)(2,1)}, bf16[2304,64]{0,1:T(8,128)(2,1)S(1)}, u32[]{:S(2)}) copy-start(bf16[2304,64]{0,1:T(8,128)(2,1)S(1)} %reshape.168) | copy-start | bytes 884740
  38.9 3.3 %copy-start.5 = (bf16[2304,64]{0,1:T(8,128)(2,1)}, bf16[2304,64]{0,1:T(8,128)(2,1)S(1)}, u32[]{:S(2)}) copy-start(bf16[2304,64]{0,1:T(8,128)(2,1)S(1)} %reshape.167) | copy-start | bytes 884740
  40.0 8.2 %copy-start.43 = (f32[64]{0:T(128)S(1)}, f32[64]{0:T(128)}, u32[]{:S(2)}) copy-start(f32[64]{0:T(128)} %param.17) | copy-start | bytes 772
  40.0 8.2 %copy-start.44 = (f32[64]{0:T(128)S(1)}, f32[64]{0:T(128)}, u32[]{:S(2)}) copy-start(f32[64]{0:T(128)} %param.18) | copy-start | bytes 772
  42.2 6.0 %copy-start.2 = (f32[2304,64]{0,1:T(8,128)}, f32[2304,64]{0,1:T(8,128)S(1)}, u32[]{:S(2)}) copy-start(f32[2304,64]{0,1:T(8,128)S(1)} %get-tuple-element.84) | copy-start | bytes 1769476
  48.2 7.4 %copy-start.33 = (f32[256]{0:T(256)S(1)}, f32[256]{0:T(256)}, u32[]{:S(2)}) copy-start(f32[256]{0:T(256)} %param.19) | copy-start | bytes 3076
  48.2 7.4 %copy-start.36 = (f32[256]{0:T(256)S(1)}, f32[256]{0:T(256)}, u32[]{:S(2)}) copy-start(f32[256]{0:T(256)} %param.20) | copy-start | bytes 3076
  63.1 2.3 %copy-start.3 = (f32[2304,64]{0,1:T(8,128)S(1)}, f32[2304,64]{0,1:T(8,128)}, u32[]{:S(2)}) copy-start(f32[2304,64]{0,1:T(8,128)} %copy-done.2) | copy-start | bytes 1769476
  65.8 4.1 %copy-start.4 = (f32[2304,64]{0,1:T(8,128)S(1)}, f32[2304,64]{0,1:T(8,128)}, u32[]{:S(2)}) copy-start(f32[2304,64]{0,1:T(8,128)} %copy-done.2) | copy-start | bytes 1769476
  65.8 5.6 %copy-start.10 = (bf16[2304,64]{0,1:T(8,128)(2,1)S(1)}, bf16[2304,64]{0,1:T(8,128)(2,1)}, u32[]{:S(2)}) copy-start(bf16[2304,64]{0,1:T(8,128)(2,1)} %copy-done.9) | copy-start | bytes 884740
  67.3 4.5 %copy-start.16 = (bf16[2304,64]{0,1:T(8,128)(2,1)S(1)}, bf16[2304,64]{0,1:T(8,128)(2,1)}, u32[]{:S(2)}) copy-start(bf16[2304,64]{0,1:T(8,128)(2,1)} %copy-done.15) | copy-start | bytes 884740
  67.3 4.7 %copy-start.14 = (bf16[2304,64]{0,1:T(8,128)(2,1)S(1)}, bf16[2304,64]{0,1:T(8,128)(2,1)}, u32[]{:S(2)}) copy-start(bf16[2304,64]{0,1:T(8,128)(2,1)} %copy-done.13) | copy-start | bytes 884740
  67.3 5.0 %copy-start.12 = (bf16[2304,64]{0,1:T(8,128)(2,1)S(1)}, bf16[2304,64]{0,1:T(8,128)(2,1)}, u32[]{:S(2)}) copy-start(bf16[2304,64]{0,1:T(8,128)(2,1)} %copy-done.11) | copy-start | bytes 884740
  69.9 2.8 %copy-start.20 = (bf16[2304,64]{0,1:T(8,128)(2,1)S(1)}, bf16[2304,64]{0,1:T(8,128)(2,1)}, u32[]{:S(2)}) copy-start(bf16[2304,64]{0,1:T(8,128)(2,1)} %copy-done.19) | copy-start | bytes 884740
  69.9 3.0 %copy-start.18 = (bf16[2304,64]{0,1:T(8,128)(2,1)S(1)}, bf16[2304,64]{0,1:T(8,128)(2,1)}, u32[]{:S(2)}) copy-start(bf16[2304,64]{0,1:T(8,128)(2,1)} %copy-done.17) | copy-start | bytes 884740
  71.4 1.8 copy-start.6
  71.8 5.6 %copy-start.8 = (bf16[2304,64]{0,1:T(8,128)(2,1)S(1)}, bf16[2304,64]{0,1:T(8,128)(2,1)}, u32[]{:S(2)}) copy-start(bf16[2304,64]{0,1:T(8,128)(2,1)} %copy-done.7) | copy-start | bytes 884740
  73.6 7.4 %collective-permute-start.2 = (bf16[2,288,64]{1,0,2:T(2,128)(2,1)S(1)}, bf16[2,288,64]{1,0,2:T(2,128)(2,1)S(1)}, u32[]{:S(2)}, u32[]{:S(2)}) collective-permute-start(bf16[2,288,64]{1,0,2:T(2,128)(2,1)S(1)} %slice.212), channel_id=1, source_target_pairs={{0,1},{2,3},{4,5},{6,7},{8,9},{10,11},{12,13},{14,15},{16,17},{18,... | collective-permute-start | bytes 221192 | tf_op jit(solution)/shard_map/ppermute | solution.py:14
  76.0 5.0 %collective-permute-start.3 = (bf16[2,288,64]{1,0,2:T(2,128)(2,1)S(1)}, bf16[2,288,64]{1,0,2:T(2,128)(2,1)S(1)}, u32[]{:S(2)}, u32[]{:S(2)}) collective-permute-start(bf16[2,288,64]{1,0,2:T(2,128)(2,1)S(1)} %slice.214), channel_id=1, source_target_pairs={{1,0},{3,2},{5,4},{7,6},{9,8},{11,10},{13,12},{15,14},{17,16},{19,... | collective-permute-start | bytes 221192 | tf_op jit(solution)/shard_map/ppermute | solution.py:17
  84.2 4.9 %copy-start.26 = (bf16[3,3,64,64]{2,3,1,0:T(8,128)(2,1)S(1)}, bf16[3,3,64,64]{2,3,1,0:T(8,128)(2,1)}, u32[]{:S(2)}) copy-start(bf16[3,3,64,64]{2,3,1,0:T(8,128)(2,1)} %reverse_bitcast_fusion) | copy-start | bytes 221188
  88.1 2.5 %copy-start.24 = (bf16[2304,64]{0,1:T(8,128)(2,1)S(1)}, bf16[2304,64]{0,1:T(8,128)(2,1)}, u32[]{:S(2)}) copy-start(bf16[2304,64]{0,1:T(8,128)(2,1)} %reshape.173) | copy-start | bytes 884740
  89.2 1.6 copy-start.23
  90.8 1.1 copy-start.22
  92.2 1.0 copy-start.30
  92.3 1.0 copy-start.32
  94.7 7.0 %copy-start.27 = (bf16[36864]{0:T(1024)(128)(2,1)S(1)}, bf16[36864]{0:T(1024)(128)(2,1)}, u32[]{:S(2)}) copy-start(bf16[36864]{0:T(1024)(128)(2,1)} %reshape_reshape.4) | copy-start | bytes 221188
  94.7 7.0 %copy-start.39 = (bf16[64]{0:T(256)(128)(2,1)S(1)}, bf16[64]{0:T(256)(128)(2,1)}, u32[]{:S(2)}) copy-start(bf16[64]{0:T(256)(128)(2,1)} %convert.79) | copy-start | bytes 388
  94.7 7.0 %copy-start.40 = (bf16[64]{0:T(256)(128)(2,1)S(1)}, bf16[64]{0:T(256)(128)(2,1)}, u32[]{:S(2)}) copy-start(bf16[64]{0:T(256)(128)(2,1)} %convert.80) | copy-start | bytes 388
  94.7 7.0 %copy-start.41 = (bf16[256]{0:T(256)(128)(2,1)S(1)}, bf16[256]{0:T(256)(128)(2,1)}, u32[]{:S(2)}) copy-start(bf16[256]{0:T(256)(128)(2,1)} %convert.81) | copy-start | bytes 1540
  94.8 7.0 %copy-start.42 = (bf16[256]{0:T(256)(128)(2,1)S(1)}, bf16[256]{0:T(256)(128)(2,1)}, u32[]{:S(2)}) copy-start(bf16[256]{0:T(256)(128)(2,1)} %convert.82) | copy-start | bytes 1540
  94.8 13.3 %copy-start.1 = (f32[2304,256]{1,0:T(8,128)S(1)}, f32[2304,256]{1,0:T(8,128)}, u32[]{:S(2)}) copy-start(f32[2304,256]{1,0:T(8,128)} %get-tuple-element.45) | copy-start | bytes 7077892
  94.8 13.3 %copy-start.28 = (bf16[256,64]{0,1:T(8,128)(2,1)S(1)}, bf16[256,64]{0,1:T(8,128)(2,1)}, u32[]{:S(2)}) copy-start(bf16[256,64]{0,1:T(8,128)(2,1)} %param.12) | copy-start | bytes 98308
  (3 other events, 2.6 us)
Sparse Core Ops, SparseCore 0:
  108.2 20.3 all-reduce.8
where the time goes:
time: 223 us; the launch traced here: 222 us
  blocking collectives  106 us (48%)
  local copies, waits for them, and re-layouts  29.5 us (13%)
  matrix products  23.4 us (10%)
  other arithmetic  21.6 us (10%)
  waiting for transfers between devices  19 us (9%)
  between operations  15.8 us (7%)
  starting transfers between devices  7.13 us (3%)
    psum x1, blocking collectives, shards(): share = lax.psum(share, 'dp')  78.9 us
    unnamed x2, waiting for transfers between devices  19 us
    dot_general x18, matrix products, dilated(): jnp.dot(window, kernel[tap_row, tap_col], preferred_element_type=jnp.floa...  12.7 us
    reshape x16, local copies, waits for them, and re-layouts, dilated(): window = padded[2 * tap_row:2 * tap_row + rows, 2 * tap_col:2 * tap_col +...  12.4 us
    psum x3, blocking collectives, backnorm(): grad_sum, grad_cross = lax.psum((local_sum, local_cross), 'space')  8.68 us
    psum x3, blocking collectives, normalize(): average = lax.psum(jnp.sum(pre, 0), 'space') / count  8.36 us
    psum x3, blocking collectives, normalize(): variance = lax.psum(jnp.sum(centred * centred, 0), 'space') / count  7.59 us
    concatenate x1, local copies, waits for them, and re-layouts, shards(): flat_grads = jnp.concatenate([item.reshape(-1) for item in parts_list])  6.29 us
  transfers between devices with their start and end apart: 5, of which 1 were waited for; matrix products, arithmetic and copies ran while one was open for 3% of the time, Pallas kernels for 0%

commit v1 on v0

--- a/solution.py
+++ b/solution.py
@@ -142,7 +142,9 @@
     share = lax.psum_scatter(
         flat_grads.astype(jnp.bfloat16), "space", scatter_dimension=0, tiled=True
     ).astype(jnp.float32)
-    share = lax.psum(share, "dp")
+    share = share
+    for hop in (1, 2, 4, 8):
+        share = share + lax.ppermute(share, "dp", [(dev, dev ^ hop) for dev in range(16)])
     whole = lax.all_gather(share.astype(jnp.bfloat16), "space", axis=0, tiled=True).astype(
         share.dtype
     )

time: 223 us -> 168 us (0.75)
  blocking collectives: 106 us -> 25.9 us
  waiting for transfers between devices: 19 us -> 33.8 us
  starting transfers between devices: 7.13 us -> 15.6 us
    psum x1 -> x0, blocking collectives: 78.9 us -> none  [shards(): share = lax.psum(share, 'dp')]
    ppermute x0 -> x4, waiting for transfers between devices: none -> 14 us  [shards(): lax.ppermute(share, 'dp', [(dev, dev ^ hop) for dev in range(16)])]
    ppermute x0 -> x4, starting transfers between devices: none -> 8.44 us  [shards(): lax.ppermute(share, 'dp', [(dev, dev ^ hop) for dev in range(16)])]
  transfers between devices with their start and end apart: 5 -> 9, of which waited for: 1 -> 6; matrix products, arithmetic and copies ran while one was open for 3% -> 4% of each run, Pallas kernels for 0% -> 0%
where the time goes in v1:
time: 168 us; the launch traced here: 167 us
  waiting for transfers between devices  33.8 us (20%)
  local copies, waits for them, and re-layouts  29.6 us (18%)
  blocking collectives  25.9 us (15%)
  matrix products  23.4 us (14%)
  other arithmetic  22.7 us (14%)
  between operations  15.8 us (9%)
  starting transfers between devices  15.6 us (9%)
    unnamed x2, waiting for transfers between devices  19.2 us
    ppermute x4, waiting for transfers between devices, shards(): lax.ppermute(share, 'dp', [(dev, dev ^ hop) for dev in range(16)])  14 us
    dot_general x18, matrix products, dilated(): jnp.dot(window, kernel[tap_row, tap_col], preferred_element_type=jnp.floa...  12.7 us
    reshape x16, local copies, waits for them, and re-layouts, dilated(): window = padded[2 * tap_row:2 * tap_row + rows, 2 * tap_col:2 * tap_col +...  12.4 us
    psum x3, blocking collectives, backnorm(): grad_sum, grad_cross = lax.psum((local_sum, local_cross), 'space')  8.55 us
    ppermute x4, starting transfers between devices, shards(): lax.ppermute(share, 'dp', [(dev, dev ^ hop) for dev in range(16)])  8.44 us
    psum x3, blocking collectives, normalize(): average = lax.psum(jnp.sum(pre, 0), 'space') / count  7.79 us
    psum x3, blocking collectives, normalize(): variance = lax.psum(jnp.sum(centred * centred, 0), 'space') / count  7.59 us
  transfers between devices with their start and end apart: 9, of which 6 were waited for; matrix products, arithmetic and copies ran while one was open for 4% of the time, Pallas kernels for 0%

profile of v1, /device:TPU:0, one launch (start us, length us, event | category | flops | bytes accessed | tf_op | source)
XLA Modules:
  0.0 166.9 jit_solution(12652808267615334161)
XLA Ops:
  7.3 1.9 %fusion.60 = (f32[64]{0:T(128)S(1)}, f32[2304,64]{0,1:T(8,128)S(1)}) fusion(bf16[2304,256]{1,0:T(8,128)(2,1)} %bitcast.202, bf16[256,64]{0,1:T(8,128)(2,1)} %param.12), kind=kOutput, calls=%fused_computation.150 | convolution fusion | flops 75644864 | bytes 1802496 | tf_op jit(solution)/shard_map/dot_general | solution.py:87
  9.2 2.6 %psum.84 = f32[64]{0:T(128)S(1)} all-reduce(f32[64]{0:T(128)S(1)} %get-tuple-element.81), channel_id=1, replica_groups=mesh['dp'=16,'space'=2] {'space'}, use_global_device_ids=true, to_apply=%region_1.0 | all-reduce | flops 64 | bytes 512 | tf_op jit(solution)/shard_map/psum | solution.py:32
  12.1 2.5 %psum.85 = f32[64]{0:T(128)S(1)} all-reduce(f32[64]{0:T(128)S(1)} %multiply_reduce_fusion.5), channel_id=1, replica_groups=mesh['dp'=16,'space'=2] {'space'}, use_global_device_ids=true, to_apply=%region_3.0 | all-reduce | flops 64 | bytes 512 | tf_op jit(solution)/shard_map/psum | solution.py:34
  16.3 2.3 %collective-permute-start = (bf16[2,288,64]{1,0,2:T(2,128)(2,1)S(1)}, bf16[2,288,64]{1,0,2:T(2,128)(2,1)S(1)}, u32[]{:S(2)}, u32[]{:S(2)}) collective-permute-start(bf16[2,288,64]{1,0,2:T(2,128)(2,1)S(1)} %slice.191), channel_id=1, source_target_pairs={{0,1},{2,3},{4,5},{6,7},{8,9},{10,11},{12,13},{14,15},{16,17},{18,... | collective-permute-start | bytes 221192 | tf_op jit(solution)/shard_map/ppermute | solution.py:14
  18.7 1.3 collective-permute-start.1
  22.9 1.8 %fusion.57 = (bf16[8,288,64]{1,0,2:T(8,128)(2,1)S(1)}, bf16[8,288,64]{1,0,2:T(8,128)(2,1)}, bf16[8,288,64]{1,0,2:T(8,128)(2,1)}, bf16[8,288,64]{1,0,2:T(8,128)(2...) fusion(bf16[12,292,64]{1,0,2:T(8,128)(2,1)S(1)} %select_maximum_fusion.2), kind=kLoop, calls=%fused_computation.147 | loop fusion | bytes 3538944 | tf_op jit(solution)/shard_map/slice | solution.py:54
  25.3 1.1 pad_maximum_fusion.2
  26.8 1.4 reshape.163
  28.2 1.4 reshape.164
  31.8 1.1 convolution_add_fusion.12
  33.9 1.3 reshape.165
  36.9 1.3 reshape.167
  38.3 1.0 convolution_add_fusion.10
  40.4 1.1 fusion.61
  41.5 2.7 %psum.86 = f32[64]{0:T(128)S(1)} all-reduce(f32[64]{0:T(128)S(1)} %get-tuple-element.83), channel_id=1, replica_groups=mesh['dp'=16,'space'=2] {'space'}, use_global_device_ids=true, to_apply=%region_5.6 | all-reduce | flops 64 | bytes 512 | tf_op jit(solution)/shard_map/psum | solution.py:32
  44.5 2.5 %psum.87 = f32[64]{0:T(128)S(1)} all-reduce(f32[64]{0:T(128)S(1)} %multiply_reduce_fusion.4), channel_id=1, replica_groups=mesh['dp'=16,'space'=2] {'space'}, use_global_device_ids=true, to_apply=%region_7.8 | all-reduce | flops 64 | bytes 512 | tf_op jit(solution)/shard_map/psum | solution.py:34
  47.0 1.9 %fusion.62 = (f32[256]{0:T(256)S(1)}, f32[2304,256]{1,0:T(8,128)S(1)}) fusion(bf16[64,256]{1,0:T(8,128)(2,1)S(1)} %copy-done, f32[2304,64]{0,1:T(8,128)} %copy-done.2, f32[64]{0:T(128)S(1)} %copy-done.44, f32[64]{0:T(128)S(1)} %get-tuple-element.80, f32[64]{0:T(128)S(1)} %broadcast_multiply_fusion.4, f32[64]{0:T(128)S(1)} %copy-done.43), kind=kOutput, calls=%fused_computation.152 | convolution fusion | flops 77414144 | bytes 2983936 | tf_op jit(solution)/shard_map/dot_general | solution.py:95
  48.8 2.5 %psum.88 = f32[256]{0:T(256)S(1)} all-reduce(f32[256]{0:T(256)S(1)} %get-tuple-element.85), channel_id=1, replica_groups=mesh['dp'=16,'space'=2] {'space'}, use_global_device_ids=true, to_apply=%region_9.10 | all-reduce | flops 256 | bytes 2048 | tf_op jit(solution)/shard_map/psum | solution.py:32
  51.7 2.6 %psum.89 = f32[256]{0:T(256)S(1)} all-reduce(f32[256]{0:T(256)S(1)} %multiply_reduce_fusion.1), channel_id=1, replica_groups=mesh['dp'=16,'space'=2] {'space'}, use_global_device_ids=true, to_apply=%region_11.12 | all-reduce | flops 256 | bytes 2048 | tf_op jit(solution)/shard_map/psum | solution.py:34
  54.3 5.1 %fusion.53 = (f32[256]{0:T(256)S(1)}, f32[256]{0:T(256)S(1)}, f32[2304,256]{1,0:T(8,128)}, bf16[2304,256]{1,0:T(8,128)(2,1)}) fusion(f32[256]{0:T(256)S(1)} %get-tuple-element.76, f32[2304,256]{1,0:T(8,128)S(1)} %get-tuple-element.86, f32[256]{0:T(256)S(1)} %broadcast_multiply_fusion.1, bf16[1,8,288,256]{3,2,1,0:T(8,128)(2,1)} %param.11, ...), kind=kLoop, calls=%fused_computation.143 | loop fusion | flops 11795968 | bytes 8263680 | tf_op jit(solution)/shard_map/reduce_sum | solution.py:41
  59.4 2.5 %all-reduce.5 = (f32[256]{0:T(256)S(1)}, f32[256]{0:T(256)S(1)}) all-reduce(f32[256]{0:T(256)S(1)} %get-tuple-element.34, f32[256]{0:T(256)S(1)} %get-tuple-element.33), channel_id=1, replica_groups=mesh['dp'=16,'space'=2] {'space'}, use_global_device_ids=true, to_apply=%region_15.16 | all-reduce | flops 512 | bytes 4096 | tf_op jit(solution)/shard_map/psum | solution.py:43
  61.9 2.3 %multiply_convert_fusion = bf16[2304,256]{1,0:T(8,128)(2,1)S(1)} fusion(f32[2304,256]{1,0:T(8,128)} %get-tuple-element.45, f32[2304,256]{1,0:T(8,128)S(1)} %get-tuple-element.86, f32[256]{0:T(256)S(1)} %get-tuple-element.43, f32[256]{0:T(256)S(1)} %broadcast_multiply_fusion, f32[256]{0:T(256)S(1)} %get-tuple-element.75, f32[256]{0:T(256)S(1)} %get-tuple-element.76, ...), kind=kLoop, calls=%fused_computation.23 | loop fusion | flops 4718592 | bytes 5903360 | tf_op jit(solution)/shard_map/convert_element_type | solution.py:44
  64.6 1.5 fusion.55
  66.1 2.6 %all-reduce.4 = (f32[64]{0:T(128)S(1)}, f32[64]{0:T(128)S(1)}) all-reduce(f32[64]{0:T(128)S(1)} %get-tuple-element.38, f32[64]{0:T(128)S(1)} %get-tuple-element.37), channel_id=1, replica_groups=mesh['dp'=16,'space'=2] {'space'}, use_global_device_ids=true, to_apply=%region_19.20 | all-reduce | flops 128 | bytes 1024 | tf_op jit(solution)/shard_map/psum | solution.py:43
  68.7 1.5 multiply_convert_fusion.3
  72.4 2.3 %collective-permute-start.2 = (bf16[2,288,64]{1,0,2:T(2,128)(2,1)S(1)}, bf16[2,288,64]{1,0,2:T(2,128)(2,1)S(1)}, u32[]{:S(2)}, u32[]{:S(2)}) collective-permute-start(bf16[2,288,64]{1,0,2:T(2,128)(2,1)S(1)} %slice.212), channel_id=1, source_target_pairs={{0,1},{2,3},{4,5},{6,7},{8,9},{10,11},{12,13},{14,15},{16,17},{18,... | collective-permute-start | bytes 221192 | tf_op jit(solution)/shard_map/ppermute | solution.py:14
  74.8 1.3 collective-permute-start.3
  79.8 1.1 pad_maximum_fusion
  83.0 1.5 fusion.56
  84.6 1.3 reshape.171
  86.9 1.1 reshape.174
  88.2 1.2 convolution_add_fusion.7
  92.1 1.4 fusion.54
  93.6 3.5 %all-reduce.3 = (f32[64]{0:T(128)S(1)}, f32[64]{0:T(128)S(1)}) all-reduce(f32[64]{0:T(128)S(1)} %get-tuple-element.36, f32[64]{0:T(128)S(1)} %get-tuple-element.35), channel_id=1, replica_groups=mesh['dp'=16,'space'=2] {'space'}, use_global_device_ids=true, to_apply=%region_23.24 | all-reduce | flops 128 | bytes 1024 | tf_op jit(solution)/shard_map/psum | solution.py:43
  97.1 1.6 multiply_convert_fusion.2
  98.7 1.6 fusion.5
  100.6 6.3 %concatenate.28 = bf16[70400]{0:T(1024)(128)(2,1)} concatenate(bf16[16384]{0:T(1024)(128)(2,1)S(1)} %reshape.180, bf16[36864]{0:T(1024)(128)(2,1)S(1)} %copy-done.27, bf16[16384]{0:T(1024)(128)(2,1)S(1)} %bitcast.206, bf16[64]{0:T(256)(128)(2,1)S(1)} %convert.77, bf16[64]{0:T(256)(128)(2,1)S(1)} %convert.78, bf16[64]{0:T(256)(128)(2,1)S(1)} %copy-done.39, ...), dimensions={0} | concatenate | bytes 281600 | tf_op jit(solution)/shard_map/concatenate | solution.py:137
  108.1 19.2 %all-reduce.8.cloned.1.call-done = bf16[70400]{0:T(1024)(128)(2,1)} async-done(((bf16[70400]{0:T(1024)(128)(2,1)}), bf16[70400]{0:T(1024)(128)(2,1)}) %all-reduce.8.cloned.1.call-update) | async-done | bytes 140816
  128.3 1.9 %collective-permute-start.4 = (f32[35200]{0:T(1024)S(1)}, f32[35200]{0:T(1024)S(1)}, u32[]{:S(2)}, u32[]{:S(2)}) collective-permute-start(f32[35200]{0:T(1024)S(1)} %dynamic-slice_convert_fusion), channel_id=1, source_target_pairs={{0,2},{2,0},{4,6},{6,4},{8,10},{10,8},{12,14},{14,12},{16,18},{18,... | collective-permute-start | bytes 422408 | tf_op jit(solution)/shard_map/ppermute | solution.py:147
  130.2 4.2 %collective-permute-done.4 = f32[35200]{0:T(1024)S(1)} collective-permute-done((f32[35200]{0:T(1024)S(1)}, f32[35200]{0:T(1024)S(1)}, u32[]{:S(2)}, u32[]{:S(2)}) %collective-permute-start.4) | collective-permute-done | bytes 140832 | tf_op jit(solution)/shard_map/ppermute | solution.py:147
  135.4 1.8 %collective-permute-start.5 = (f32[35200]{0:T(1024)S(1)}, f32[35200]{0:T(1024)S(1)}, u32[]{:S(2)}, u32[]{:S(2)}) collective-permute-start(f32[35200]{0:T(1024)S(1)} %fusion.26), channel_id=1, source_target_pairs={{0,4},{2,6},{4,0},{6,2},{8,12},{10,14},{12,8},{14,10},{16,20},{18,... | collective-permute-start | bytes 422408 | tf_op jit(solution)/shard_map/ppermute | solution.py:147
  137.2 3.4 %collective-permute-done.5 = f32[35200]{0:T(1024)S(1)} collective-permute-done((f32[35200]{0:T(1024)S(1)}, f32[35200]{0:T(1024)S(1)}, u32[]{:S(2)}, u32[]{:S(2)}) %collective-permute-start.5) | collective-permute-done | bytes 140832 | tf_op jit(solution)/shard_map/ppermute | solution.py:147
  140.6 1.8 %collective-permute-start.6 = (f32[35200]{0:T(1024)S(1)}, f32[35200]{0:T(1024)S(1)}, u32[]{:S(2)}, u32[]{:S(2)}) collective-permute-start(f32[35200]{0:T(1024)S(1)} %add.188), channel_id=1, source_target_pairs={{0,8},{2,10},{4,12},{6,14},{8,0},{10,2},{12,4},{14,6},{16,24},{18,... | collective-permute-start | bytes 422408 | tf_op jit(solution)/shard_map/ppermute | solution.py:147
  142.4 3.4 %collective-permute-done.6 = f32[35200]{0:T(1024)S(1)} collective-permute-done((f32[35200]{0:T(1024)S(1)}, f32[35200]{0:T(1024)S(1)}, u32[]{:S(2)}, u32[]{:S(2)}) %collective-permute-start.6) | collective-permute-done | bytes 140832 | tf_op jit(solution)/shard_map/ppermute | solution.py:147
  145.8 3.0 %collective-permute-start.7 = (f32[35200]{0:T(1024)S(1)}, f32[35200]{0:T(1024)S(1)}, u32[]{:S(2)}, u32[]{:S(2)}) collective-permute-start(f32[35200]{0:T(1024)S(1)} %add.189), channel_id=1, source_target_pairs={{0,16},{2,18},{4,20},{6,22},{8,24},{10,26},{12,28},{14,30},{16,0},... | collective-permute-start | bytes 422408 | tf_op jit(solution)/shard_map/ppermute | solution.py:147
  148.7 1.5 fusion
  150.2 3.1 %collective-permute-done.7 = f32[35200]{0:T(1024)S(1)} collective-permute-done((f32[35200]{0:T(1024)S(1)}, f32[35200]{0:T(1024)S(1)}, u32[]{:S(2)}, u32[]{:S(2)}) %collective-permute-start.7) | collective-permute-done | bytes 140832 | tf_op jit(solution)/shard_map/ppermute | solution.py:147
  153.5 2.0 %all-gather = bf16[2,1,35200]{2,1,0:T(2,128)(2,1)S(1)} all-gather(bf16[1,1,35200]{2,1,0:T(2,128)(2,1)S(1)} %reshape.183), channel_id=1, replica_groups=mesh['dp'=16,'space'=2] {'space'}, dimensions={0}, use_global_device_ids=true | all-gather | bytes 211200 | tf_op jit(solution)/shard_map/all_gather | solution.py:148
  (182 shorter events, 32.1 us)
Async XLA Ops:
  7.2 39.8 %copy-start = (bf16[64,256]{1,0:T(8,128)(2,1)S(1)}, bf16[64,256]{1,0:T(8,128)(2,1)}, u32[]{:S(2)}) copy-start(bf16[64,256]{1,0:T(8,128)(2,1)} %param.14) | copy-start | bytes 98308
  7.2 7.3 %copy-start.34 = (f32[64]{0:T(128)S(1)}, f32[64]{0:T(128)}, u32[]{:S(2)}) copy-start(f32[64]{0:T(128)} %param.15) | copy-start | bytes 772
  7.2 8.4 %copy-start.37 = (f32[64]{0:T(128)S(1)}, f32[64]{0:T(128)}, u32[]{:S(2)}) copy-start(f32[64]{0:T(128)} %param.16) | copy-start | bytes 772
  7.2 13.4 %copy-start.25 = (bf16[3,3,64,64]{3,2,1,0:T(8,128)(2,1)S(1)}, bf16[3,3,64,64]{3,2,1,0:T(8,128)(2,1)}, u32[]{:S(2)}) copy-start(bf16[3,3,64,64]{3,2,1,0:T(8,128)(2,1)} %param.13) | copy-start | bytes 221188
  7.2 120.1 %all-reduce.8.cloned.1.call-start = ((), (), s32[]{:S(2)}) async-start(), calls=%async_computation | async-start | bytes 282624
  11.8 3.2 %copy-start.29 = (f32[64]{0:T(128)}, f32[64]{0:T(128)S(1)}, u32[]{:S(2)}) copy-start(f32[64]{0:T(128)S(1)} %broadcast_multiply_fusion.5) | copy-start | bytes 772
  16.3 5.0 %collective-permute-start = (bf16[2,288,64]{1,0,2:T(2,128)(2,1)S(1)}, bf16[2,288,64]{1,0,2:T(2,128)(2,1)S(1)}, u32[]{:S(2)}, u32[]{:S(2)}) collective-permute-start(bf16[2,288,64]{1,0,2:T(2,128)(2,1)S(1)} %slice.191), channel_id=1, source_target_pairs={{0,1},{2,3},{4,5},{6,7},{8,9},{10,11},{12,13},{14,15},{16,17},{18,... | collective-permute-start | bytes 221192 | tf_op jit(solution)/shard_map/ppermute | solution.py:14
  18.7 3.2 %collective-permute-start.1 = (bf16[2,288,64]{1,0,2:T(2,128)(2,1)S(1)}, bf16[2,288,64]{1,0,2:T(2,128)(2,1)S(1)}, u32[]{:S(2)}, u32[]{:S(2)}) collective-permute-start(bf16[2,288,64]{1,0,2:T(2,128)(2,1)S(1)} %slice.193), channel_id=1, source_target_pairs={{1,0},{3,2},{5,4},{7,6},{9,8},{11,10},{13,12},{15,14},{17,16},{19,... | collective-permute-start | bytes 221192 | tf_op jit(solution)/shard_map/ppermute | solution.py:17
  25.0 5.7 %copy-start.9 = (bf16[2304,64]{0,1:T(8,128)(2,1)}, bf16[2304,64]{0,1:T(8,128)(2,1)S(1)}, u32[]{:S(2)}) copy-start(bf16[2304,64]{0,1:T(8,128)(2,1)S(1)} %reshape.161) | copy-start | bytes 884740
  26.8 6.1 %copy-start.15 = (bf16[2304,64]{0,1:T(8,128)(2,1)}, bf16[2304,64]{0,1:T(8,128)(2,1)S(1)}, u32[]{:S(2)}) copy-start(bf16[2304,64]{0,1:T(8,128)(2,1)S(1)} %reshape.162) | copy-start | bytes 884740
  28.2 4.6 %copy-start.13 = (bf16[2304,64]{0,1:T(8,128)(2,1)}, bf16[2304,64]{0,1:T(8,128)(2,1)S(1)}, u32[]{:S(2)}) copy-start(bf16[2304,64]{0,1:T(8,128)(2,1)S(1)} %reshape.163) | copy-start | bytes 884740
  29.7 4.2 %copy-start.11 = (bf16[2304,64]{0,1:T(8,128)(2,1)}, bf16[2304,64]{0,1:T(8,128)(2,1)S(1)}, u32[]{:S(2)}) copy-start(bf16[2304,64]{0,1:T(8,128)(2,1)S(1)} %reshape.164) | copy-start | bytes 884740
  31.8 3.8 %copy-start.21 = (bf16[8,288,64]{1,0,2:T(8,128)(2,1)S(1)}, bf16[8,288,64]{1,0,2:T(8,128)(2,1)}, u32[]{:S(2)}) copy-start(bf16[8,288,64]{1,0,2:T(8,128)(2,1)} %get-tuple-element.58) | copy-start | bytes 884740
  35.2 5.2 %copy-start.19 = (bf16[2304,64]{0,1:T(8,128)(2,1)}, bf16[2304,64]{0,1:T(8,128)(2,1)S(1)}, u32[]{:S(2)}) copy-start(bf16[2304,64]{0,1:T(8,128)(2,1)S(1)} %reshape.165) | copy-start | bytes 884740
  35.5 3.8 %copy-start.17 = (bf16[2304,64]{0,1:T(8,128)(2,1)}, bf16[2304,64]{0,1:T(8,128)(2,1)S(1)}, u32[]{:S(2)}) copy-start(bf16[2304,64]{0,1:T(8,128)(2,1)S(1)} %reshape.166) | copy-start | bytes 884740
  35.9 3.4 %copy-start.7 = (bf16[2304,64]{0,1:T(8,128)(2,1)}, bf16[2304,64]{0,1:T(8,128)(2,1)S(1)}, u32[]{:S(2)}) copy-start(bf16[2304,64]{0,1:T(8,128)(2,1)S(1)} %reshape.168) | copy-start | bytes 884740
  38.2 3.3 %copy-start.5 = (bf16[2304,64]{0,1:T(8,128)(2,1)}, bf16[2304,64]{0,1:T(8,128)(2,1)S(1)}, u32[]{:S(2)}) copy-start(bf16[2304,64]{0,1:T(8,128)(2,1)S(1)} %reshape.167) | copy-start | bytes 884740
  39.3 7.6 %copy-start.43 = (f32[64]{0:T(128)S(1)}, f32[64]{0:T(128)}, u32[]{:S(2)}) copy-start(f32[64]{0:T(128)} %param.17) | copy-start | bytes 772
  39.3 7.6 %copy-start.44 = (f32[64]{0:T(128)S(1)}, f32[64]{0:T(128)}, u32[]{:S(2)}) copy-start(f32[64]{0:T(128)} %param.18) | copy-start | bytes 772
  41.5 5.4 %copy-start.2 = (f32[2304,64]{0,1:T(8,128)}, f32[2304,64]{0,1:T(8,128)S(1)}, u32[]{:S(2)}) copy-start(f32[2304,64]{0,1:T(8,128)S(1)} %get-tuple-element.84) | copy-start | bytes 1769476
  47.0 7.4 %copy-start.33 = (f32[256]{0:T(256)S(1)}, f32[256]{0:T(256)}, u32[]{:S(2)}) copy-start(f32[256]{0:T(256)} %param.19) | copy-start | bytes 3076
  47.0 7.4 %copy-start.36 = (f32[256]{0:T(256)S(1)}, f32[256]{0:T(256)}, u32[]{:S(2)}) copy-start(f32[256]{0:T(256)} %param.20) | copy-start | bytes 3076
  61.9 2.3 %copy-start.3 = (f32[2304,64]{0,1:T(8,128)S(1)}, f32[2304,64]{0,1:T(8,128)}, u32[]{:S(2)}) copy-start(f32[2304,64]{0,1:T(8,128)} %copy-done.2) | copy-start | bytes 1769476
  64.6 4.1 %copy-start.4 = (f32[2304,64]{0,1:T(8,128)S(1)}, f32[2304,64]{0,1:T(8,128)}, u32[]{:S(2)}) copy-start(f32[2304,64]{0,1:T(8,128)} %copy-done.2) | copy-start | bytes 1769476
  64.6 5.6 %copy-start.10 = (bf16[2304,64]{0,1:T(8,128)(2,1)S(1)}, bf16[2304,64]{0,1:T(8,128)(2,1)}, u32[]{:S(2)}) copy-start(bf16[2304,64]{0,1:T(8,128)(2,1)} %copy-done.9) | copy-start | bytes 884740
  66.1 4.5 %copy-start.16 = (bf16[2304,64]{0,1:T(8,128)(2,1)S(1)}, bf16[2304,64]{0,1:T(8,128)(2,1)}, u32[]{:S(2)}) copy-start(bf16[2304,64]{0,1:T(8,128)(2,1)} %copy-done.15) | copy-start | bytes 884740
  66.1 4.7 %copy-start.14 = (bf16[2304,64]{0,1:T(8,128)(2,1)S(1)}, bf16[2304,64]{0,1:T(8,128)(2,1)}, u32[]{:S(2)}) copy-start(bf16[2304,64]{0,1:T(8,128)(2,1)} %copy-done.13) | copy-start | bytes 884740
  66.1 5.0 %copy-start.12 = (bf16[2304,64]{0,1:T(8,128)(2,1)S(1)}, bf16[2304,64]{0,1:T(8,128)(2,1)}, u32[]{:S(2)}) copy-start(bf16[2304,64]{0,1:T(8,128)(2,1)} %copy-done.11) | copy-start | bytes 884740
  68.7 2.8 %copy-start.20 = (bf16[2304,64]{0,1:T(8,128)(2,1)S(1)}, bf16[2304,64]{0,1:T(8,128)(2,1)}, u32[]{:S(2)}) copy-start(bf16[2304,64]{0,1:T(8,128)(2,1)} %copy-done.19) | copy-start | bytes 884740
  68.7 3.0 %copy-start.18 = (bf16[2304,64]{0,1:T(8,128)(2,1)S(1)}, bf16[2304,64]{0,1:T(8,128)(2,1)}, u32[]{:S(2)}) copy-start(bf16[2304,64]{0,1:T(8,128)(2,1)} %copy-done.17) | copy-start | bytes 884740
  70.2 1.8 %copy-start.6 = (bf16[2304,64]{0,1:T(8,128)(2,1)S(1)}, bf16[2304,64]{0,1:T(8,128)(2,1)}, u32[]{:S(2)}) copy-start(bf16[2304,64]{0,1:T(8,128)(2,1)} %copy-done.5) | copy-start | bytes 884740
  70.6 5.6 %copy-start.8 = (bf16[2304,64]{0,1:T(8,128)(2,1)S(1)}, bf16[2304,64]{0,1:T(8,128)(2,1)}, u32[]{:S(2)}) copy-start(bf16[2304,64]{0,1:T(8,128)(2,1)} %copy-done.7) | copy-start | bytes 884740
  72.4 7.4 %collective-permute-start.2 = (bf16[2,288,64]{1,0,2:T(2,128)(2,1)S(1)}, bf16[2,288,64]{1,0,2:T(2,128)(2,1)S(1)}, u32[]{:S(2)}, u32[]{:S(2)}) collective-permute-start(bf16[2,288,64]{1,0,2:T(2,128)(2,1)S(1)} %slice.212), channel_id=1, source_target_pairs={{0,1},{2,3},{4,5},{6,7},{8,9},{10,11},{12,13},{14,15},{16,17},{18,... | collective-permute-start | bytes 221192 | tf_op jit(solution)/shard_map/ppermute | solution.py:14
  74.8 5.0 %collective-permute-start.3 = (bf16[2,288,64]{1,0,2:T(2,128)(2,1)S(1)}, bf16[2,288,64]{1,0,2:T(2,128)(2,1)S(1)}, u32[]{:S(2)}, u32[]{:S(2)}) collective-permute-start(bf16[2,288,64]{1,0,2:T(2,128)(2,1)S(1)} %slice.214), channel_id=1, source_target_pairs={{1,0},{3,2},{5,4},{7,6},{9,8},{11,10},{13,12},{15,14},{17,16},{19,... | collective-permute-start | bytes 221192 | tf_op jit(solution)/shard_map/ppermute | solution.py:17
  83.0 5.0 %copy-start.26 = (bf16[3,3,64,64]{2,3,1,0:T(8,128)(2,1)S(1)}, bf16[3,3,64,64]{2,3,1,0:T(8,128)(2,1)}, u32[]{:S(2)}) copy-start(bf16[3,3,64,64]{2,3,1,0:T(8,128)(2,1)} %reverse_bitcast_fusion) | copy-start | bytes 221188
  86.9 2.5 %copy-start.24 = (bf16[2304,64]{0,1:T(8,128)(2,1)S(1)}, bf16[2304,64]{0,1:T(8,128)(2,1)}, u32[]{:S(2)}) copy-start(bf16[2304,64]{0,1:T(8,128)(2,1)} %reshape.173) | copy-start | bytes 884740
  93.5 7.0 %copy-start.27 = (bf16[36864]{0:T(1024)(128)(2,1)S(1)}, bf16[36864]{0:T(1024)(128)(2,1)}, u32[]{:S(2)}) copy-start(bf16[36864]{0:T(1024)(128)(2,1)} %reshape_reshape.4) | copy-start | bytes 221188
  93.5 7.0 %copy-start.39 = (bf16[64]{0:T(256)(128)(2,1)S(1)}, bf16[64]{0:T(256)(128)(2,1)}, u32[]{:S(2)}) copy-start(bf16[64]{0:T(256)(128)(2,1)} %convert.79) | copy-start | bytes 388
  93.5 7.0 %copy-start.40 = (bf16[64]{0:T(256)(128)(2,1)S(1)}, bf16[64]{0:T(256)(128)(2,1)}, u32[]{:S(2)}) copy-start(bf16[64]{0:T(256)(128)(2,1)} %convert.80) | copy-start | bytes 388
  93.5 7.0 %copy-start.41 = (bf16[256]{0:T(256)(128)(2,1)S(1)}, bf16[256]{0:T(256)(128)(2,1)}, u32[]{:S(2)}) copy-start(bf16[256]{0:T(256)(128)(2,1)} %convert.81) | copy-start | bytes 1540
  93.5 7.0 %copy-start.42 = (bf16[256]{0:T(256)(128)(2,1)S(1)}, bf16[256]{0:T(256)(128)(2,1)}, u32[]{:S(2)}) copy-start(bf16[256]{0:T(256)(128)(2,1)} %convert.82) | copy-start | bytes 1540
  93.6 13.3 %copy-start.45 = (u32[32]{0:T(128)S(1)}, u32[32]{0:T(128)}, u32[]{:S(2)}) copy-start(u32[32]{0:T(128)} %constant.51) | copy-start | bytes 388
  97.1 51.6 %copy-start.1 = (f32[2304,256]{1,0:T(8,128)S(1)}, f32[2304,256]{1,0:T(8,128)}, u32[]{:S(2)}) copy-start(f32[2304,256]{1,0:T(8,128)} %get-tuple-element.45) | copy-start | bytes 7077892
  97.1 51.6 %copy-start.28 = (bf16[256,64]{0,1:T(8,128)(2,1)S(1)}, bf16[256,64]{0,1:T(8,128)(2,1)}, u32[]{:S(2)}) copy-start(bf16[256,64]{0,1:T(8,128)(2,1)} %param.12) | copy-start | bytes 98308
  128.3 6.0 %collective-permute-start.4 = (f32[35200]{0:T(1024)S(1)}, f32[35200]{0:T(1024)S(1)}, u32[]{:S(2)}, u32[]{:S(2)}) collective-permute-start(f32[35200]{0:T(1024)S(1)} %dynamic-slice_convert_fusion), channel_id=1, source_target_pairs={{0,2},{2,0},{4,6},{6,4},{8,10},{10,8},{12,14},{14,12},{16,18},{18,... | collective-permute-start | bytes 422408 | tf_op jit(solution)/shard_map/ppermute | solution.py:147
  135.4 5.2 %collective-permute-start.5 = (f32[35200]{0:T(1024)S(1)}, f32[35200]{0:T(1024)S(1)}, u32[]{:S(2)}, u32[]{:S(2)}) collective-permute-start(f32[35200]{0:T(1024)S(1)} %fusion.26), channel_id=1, source_target_pairs={{0,4},{2,6},{4,0},{6,2},{8,12},{10,14},{12,8},{14,10},{16,20},{18,... | collective-permute-start | bytes 422408 | tf_op jit(solution)/shard_map/ppermute | solution.py:147
  140.6 5.2 %collective-permute-start.6 = (f32[35200]{0:T(1024)S(1)}, f32[35200]{0:T(1024)S(1)}, u32[]{:S(2)}, u32[]{:S(2)}) collective-permute-start(f32[35200]{0:T(1024)S(1)} %add.188), channel_id=1, source_target_pairs={{0,8},{2,10},{4,12},{6,14},{8,0},{10,2},{12,4},{14,6},{16,24},{18,... | collective-permute-start | bytes 422408 | tf_op jit(solution)/shard_map/ppermute | solution.py:147
  145.8 7.6 %collective-permute-start.7 = (f32[35200]{0:T(1024)S(1)}, f32[35200]{0:T(1024)S(1)}, u32[]{:S(2)}, u32[]{:S(2)}) collective-permute-start(f32[35200]{0:T(1024)S(1)} %add.189), channel_id=1, source_target_pairs={{0,16},{2,18},{4,20},{6,22},{8,24},{10,26},{12,28},{14,30},{16,0},... | collective-permute-start | bytes 422408 | tf_op jit(solution)/shard_map/ppermute | solution.py:147
  (7 other events, 7.3 us)
Sparse Core Ops, SparseCore 0:
  107.0 20.3 all-reduce.7
